TPU v7x, 256 devices: a whole 4x4x8 slice. The times are simulated.
256 devices in a mesh: head: 4 (over x), page: 64 (over y, z, core).
Axes of the slice: x: 4, y: 4, z: 8, core: 2. Of those that a mesh axis runs over, the one named last changes fastest.
Arguments:
- hidden: bfloat16 [12, 2048], P(None, 'page'), may hold values from -6 to 6
- q_weight: bfloat16 [2048, 3072], P('page', 'head'), may hold values from -0.125 to 0.125
- key_up: bfloat16 [16, 128, 512], P('head'), may hold values from -0.5 to 0.5
- value_up_weight: bfloat16 [16, 512, 128], P('head'), may hold values from -0.25 to 0.25
- out_weight: bfloat16 [2048, 2048], P('head', 'page'), may hold values from -0.125 to 0.125
- cache: bfloat16 [16, 512, 128, 576], P('head', 'page'), may hold values from -360 to 360
- page_table: int32 [16, 512], P('head', 'page'), may hold values from 0 to 511, each once within a row
- seq_pages: int32 [12], replicated, may hold values from 1 to 128, 512 in all
- keep_rows: int32 [16, 512, 64], P('head'), may hold values from 0 to 127, as said below
- fold_mass: bfloat16 [16, 512, 64], P('head'), may hold values from 0.5 to 4
- new_place: int32 [16, 512], P('head'), may hold values from 0 to 2047, as said below
- norm_gain: bfloat16 [2048], replicated, may hold values from 0.099609375 to 1.8984375
- router: bfloat16 [2048, 64], replicated, may hold values from -0.125 to 0.125
- routes: int32 [12, 6], replicated, may hold values from 0 to 63, all different within a row
- w_gate: bfloat16 [64, 2048, 1408], P('page', None, 'head'), may hold values from -0.125 to 0.125
- w_up: bfloat16 [64, 2048, 1408], P('page', None, 'head'), may hold values from -0.125 to 0.125
- w_down: bfloat16 [64, 1408, 2048], P('page', 'head'), may hold values from -0.15625 to 0.15625
Outputs:
- attn_out: bfloat16 [12, 2048], replicated
- moe_out: bfloat16 [12, 2048], replicated
- new_rows: bfloat16 [8192, 64, 576], P(('head', 'page'))
- new_mass: bfloat16 [8192, 64], P(('head', 'page'))
Inputs may be any that keep to these rules, and one draw needn't show every extreme that they name: `keep_rows`: the 64 entries of each head and page are distinct. `new_place`: for each group of heads h // 4 the places form a permutation of 0 to 2047. Among the blocks of one head group whose pages share g // 8, at most 1 have places with the same place // 32, and some reach 1.
All inputs are finite; a program needn't handle non-finite values.
Results may differ from a plain program's by a relative error of at most 0.035.
Values may be sent and summed in bfloat16 or wider, within the bound.
A program may use at most 128 MiB of HBM per device.

v0:
```python
import jax
import jax.numpy as jnp
from jax import lax
from jax.sharding import PartitionSpec as P

QK_NOPE = 128
QK_ROPE = 64
THETA = 50000.0
ROUTE_SCALE = 2.446
NORM_EPS = 1e-06


def joined_2(part, axis, combine):
    gathered = jax.tree.map(lambda a: lax.all_gather(a, axis), part)

    def take(source):
        return jax.tree.map(lambda a: lax.dynamic_index_in_dim(a, source, 0, False), gathered)

    return lax.fori_loop(
        1, lax.axis_size(axis), lambda source, state: combine(state, take(source)), take(0)
    )


def rotate_query(values, positions):
    half_dim = values.shape[-1] // 2
    freqs = THETA ** (-2.0 * jnp.arange(half_dim, dtype=jnp.float32) / values.shape[-1])
    angles = positions.astype(jnp.float32)[:, None] * freqs[None, :]
    cosine = jnp.cos(angles)[:, None, :]
    sine_v = jnp.sin(angles)[:, None, :]
    front = values[..., :half_dim]
    back = values[..., half_dim:]
    return jnp.concatenate(
        [front * cosine - back * sine_v, back * cosine + front * sine_v], axis=-1
    )


def pick_rows(one_page, row_ids):
    return one_page[row_ids]


def merge_parts(left_part, right_part):
    joined = jnp.maximum(left_part[0], right_part[0])
    left_factor = jnp.exp(left_part[0] - joined)
    right_factor = jnp.exp(right_part[0] - joined)
    return (
        joined,
        left_part[1] * left_factor + right_part[1] * right_factor,
        left_part[2] * left_factor[..., None] + right_part[2] * right_factor[..., None],
    )


def shards(
    hidden,
    q_weight,
    key_up,
    value_up_weight,
    out_weight,
    cache,
    page_table,
    seq_pages,
    keep_rows,
    fold_mass,
    new_place,
    norm_gain,
    router,
    routes,
    w_gate,
    w_up,
    w_down,
):
    heads_here = key_up.shape[0]
    pages_here = cache.shape[1]
    page_rows = cache.shape[2]
    latent_dim = cache.shape[3]
    kv_rank = key_up.shape[2]
    kept_count = keep_rows.shape[2]
    requests = hidden.shape[0]
    head_size = QK_NOPE + QK_ROPE
    groups = lax.axis_size("page")
    page_index = lax.axis_index("page")
    blocks = heads_here * pages_here
    sending_limit = (blocks + groups - 1) // groups
    first_page = page_index * pages_here
    partial_value = jnp.dot(hidden, q_weight, preferred_element_type=jnp.float32)
    queries = lax.psum(partial_value, "page").reshape(requests, heads_here, head_size)
    q_nope = queries[..., :QK_NOPE].astype(jnp.bfloat16)
    positions = seq_pages * page_rows - 1
    q_rope = rotate_query(queries[..., QK_NOPE:], positions).astype(jnp.bfloat16)
    q_latent = jnp.einsum(
        "rhn,hnk->rhk", q_nope, key_up, preferred_element_type=jnp.float32
    ).astype(jnp.bfloat16)
    q_full = jnp.concatenate([q_latent, q_rope], axis=-1)
    keep_here = lax.dynamic_slice_in_dim(keep_rows, first_page, pages_here, 1)
    mass_here = lax.dynamic_slice_in_dim(fold_mass, first_page, pages_here, 1)
    compact = jax.vmap(jax.vmap(pick_rows))(cache, keep_here)
    flat_rows = compact.reshape(heads_here, pages_here * kept_count, latent_dim)
    page_ends = jnp.cumsum(seq_pages)
    owner = jnp.sum((page_table[..., None] >= page_ends).astype(jnp.int32), axis=-1)
    row_owner = jnp.repeat(owner, kept_count, axis=1)
    in_request = row_owner[:, None, :] == jnp.arange(requests, dtype=jnp.int32)[None, :, None]
    scores = jnp.einsum(
        "rhk,hnk->hrn", q_full, flat_rows, preferred_element_type=jnp.float32
    ) * head_size ** (-0.5)
    row_max = jnp.max(jnp.where(in_request, scores, -1e30), axis=-1)
    row_mass = mass_here.reshape(heads_here, 1, pages_here * kept_count).astype(jnp.float32)
    weights = jnp.where(in_request, row_mass * jnp.exp(scores - row_max[..., None]), 0.0)
    totals = jnp.sum(weights, axis=-1)
    weighted = jnp.einsum(
        "hrn,hnk->hrk",
        weights.astype(jnp.bfloat16),
        flat_rows[..., :kv_rank],
        preferred_element_type=jnp.float32,
    )
    best, mass_sum, latent_sum = joined_2((row_max, totals, weighted), "page", merge_parts)
    latent_output = (latent_sum / mass_sum[..., None]).astype(jnp.bfloat16)
    head_result_rows = jnp.einsum(
        "usj,ujb->sub", latent_output, value_up_weight, preferred_element_type=jnp.float32
    ).astype(jnp.bfloat16)
    head_result_rows = head_result_rows.reshape(requests, heads_here * value_up_weight.shape[2])
    out_cols = jnp.dot(head_result_rows, out_weight, preferred_element_type=jnp.float32)
    col_width = out_cols.shape[1]
    padded = jnp.zeros((requests, col_width * groups), jnp.float32)
    padded = lax.dynamic_update_slice_in_dim(padded, out_cols, page_index * col_width, 1)
    attn_out = lax.psum(padded, ("head", "page")).astype(jnp.bfloat16)
    attn_wide = attn_out.astype(jnp.float32)
    mean_sq = jnp.mean(attn_wide * attn_wide, axis=-1, keepdims=True)
    normed = (attn_wide * lax.rsqrt(mean_sq + NORM_EPS) * norm_gain.astype(jnp.float32)).astype(
        jnp.bfloat16
    )
    logits = jnp.dot(normed, router, preferred_element_type=jnp.float32)
    picked = jax.nn.sigmoid(jnp.take_along_axis(logits, routes, axis=1))
    shares = ROUTE_SCALE * picked / jnp.sum(picked, axis=1, keepdims=True)
    expert_ids = jnp.arange(logits.shape[1], dtype=jnp.int32)
    combine = jnp.sum(
        jnp.where(routes[:, :, None] == expert_ids[None, None, :], shares[:, :, None], 0.0), axis=1
    )
    local_experts = w_gate.shape[0]
    combine_here = lax.dynamic_slice_in_dim(combine, page_index * local_experts, local_experts, 1)
    gate_part = jnp.einsum("rd,edf->erf", normed, w_gate, preferred_element_type=jnp.float32)
    up_part = jnp.einsum("rd,edf->erf", normed, w_up, preferred_element_type=jnp.float32)
    expert_hidden = (jax.nn.silu(gate_part) * up_part).astype(jnp.bfloat16)
    expert_outs = jnp.einsum(
        "erf,efd->erd", expert_hidden, w_down, preferred_element_type=jnp.float32
    )
    expert_terms = jnp.sum(combine_here.T[:, :, None] * expert_outs, axis=0)
    moe_out = lax.psum(expert_terms, ("head", "page")).astype(jnp.bfloat16)
    dest_all = new_place // blocks
    slot_all = new_place % blocks
    dest_here = lax.dynamic_slice_in_dim(dest_all, first_page, pages_here, 1).reshape(blocks)
    peer_ids = jnp.arange(groups, dtype=jnp.int32)
    dest_onehot = (dest_here[:, None] == peer_ids[None, :]).astype(jnp.int32)
    send_rank = jnp.sum(jnp.cumsum(dest_onehot, axis=0) * dest_onehot, axis=1) - 1
    send_col = dest_here * sending_limit + send_rank
    slot_ids = jnp.arange(groups * sending_limit, dtype=jnp.int32)
    chooser = (send_col[:, None] == slot_ids[None, :]).astype(jnp.bfloat16)

    def arrange(values):
        return (
            values.reshape(heads_here, groups, pages_here)
            .transpose(1, 0, 2)
            .reshape(groups, blocks)
        )

    to_here = arrange(dest_all) == page_index
    recv_rank = jnp.cumsum(to_here.astype(jnp.int32), axis=1) - 1
    recv_col = peer_ids[:, None] * sending_limit + recv_rank
    block_ids = jnp.arange(blocks, dtype=jnp.int32)
    by_slot = ((arrange(slot_all)[..., None] == block_ids) & to_here[..., None]).astype(
        jnp.bfloat16
    )
    by_col = (recv_col[..., None] == slot_ids).astype(jnp.bfloat16)
    unpack = jnp.einsum("sbq,sbc->qc", by_slot, by_col, preferred_element_type=jnp.float32).astype(
        jnp.bfloat16
    )
    owned = (slot_all.reshape(-1)[None, :] == block_ids[:, None]) & (
        dest_all.reshape(-1)[None, :] == page_index
    )
    new_mass = jnp.dot(
        owned.astype(jnp.bfloat16),
        fold_mass.reshape(-1, kept_count),
        preferred_element_type=jnp.float32,
    ).astype(jnp.bfloat16)
    payload = cache.reshape(blocks, page_rows * latent_dim)
    outgoing = jnp.einsum("bc,bx->cx", chooser, payload, preferred_element_type=jnp.float32).astype(
        jnp.bfloat16
    )
    arrived_rows = lax.all_to_all(
        outgoing.reshape(groups, sending_limit, page_rows, latent_dim),
        "page",
        split_axis=0,
        concat_axis=0,
        tiled=True,
    )
    placed = jnp.dot(
        unpack,
        arrived_rows.reshape(groups * sending_limit, page_rows * latent_dim),
        preferred_element_type=jnp.float32,
    ).astype(jnp.bfloat16)
    keep_new = jnp.dot(owned.astype(jnp.int32), keep_rows.reshape(-1, kept_count))
    new_rows = jax.vmap(pick_rows)(placed.reshape(blocks, page_rows, latent_dim), keep_new)
    return (attn_out, moe_out, new_rows, new_mass)


def solution(mesh):
    in_specs = (
        P(None, "page"),
        P("page", "head"),
        P("head", None, None),
        P("head", None, None),
        P("head", "page"),
        P("head", "page", None, None),
        P("head", "page"),
        P(),
        P("head", None, None),
        P("head", None, None),
        P("head", None),
        P(),
        P(),
        P(),
        P("page", None, "head"),
        P("page", None, "head"),
        P("page", "head", None),
    )
    out_specs = (P(), P(), P(("head", "page"), None, None), P(("head", "page"), None))
    return jax.shard_map(shards, mesh=mesh, in_specs=in_specs, out_specs=out_specs, check_vma=False)
```

profile of v0, /device:TPU:1, one launch (start us, length us, event | category | flops | bytes accessed | tf_op | source)
XLA Modules:
  0.0 994.9 jit_solution(4305672104055780673)
XLA Ops:
  7.3 1.1 constant_dynamic-slice_fusion.2
  8.6 7.8 copy.109
  16.6 249.7 %psum.21 = f32[12,4,192]{2,0,1:T(8,128)S(1)} all-reduce(f32[12,4,192]{2,0,1:T(8,128)S(1)} %copy.107), channel_id=1, replica_groups=mesh['head'=4,'page'=64] {'page'}, use_global_device_ids=true, to_apply=%region_2.3 | all-reduce | flops 9216 | bytes 73728 | tf_op jit(solution)/shard_map/psum | solution.py:85
  267.1 39.7 %gather_fusion = bf16[2048,576]{1,0:T(8,128)(2,1)} fusion(bf16[4,8,128,576]{3,2,1,0:T(8,128)(2,1)} %copy.109, s32[2048]{0:T(1024)S(1)} %reshape.256), kind=kCustom, calls=%fused_computation | custom fusion | bytes 4743168 | tf_op jit(solution)/shard_map/vmap(vmap())/gather | solution.py:38
  307.2 2.8 select_reduce_fusion
  310.0 1.1 fusion.3
  311.2 8.8 reshape.249
  320.5 8.7 convolution_convert_fusion
  329.2 15.5 %reshape.250 = bf16[64,1,128,576]{3,2,0,1:T(8,128)(2,1)} reshape(bf16[64,73728]{1,0:T(8,128)(2,1)} %convolution_convert_fusion) | data formatting | bytes 18874368 | tf_op jit(solution)/shard_map/reshape | solution.py:188
  344.7 13.9 %copy.123 = bf16[64,1,128,576]{2,3,1,0:T(8,128)(2,1)} copy(bf16[64,1,128,576]{3,2,0,1:T(8,128)(2,1)} %reshape.250) | data formatting | bytes 18874368 | tf_op jit(solution)/shard_map/reshape | solution.py:188
  358.6 10.9 %all-to-all-start = ((bf16[64,1,128,576]{2,3,1,0:T(8,128)(2,1)}), bf16[64,1,128,576]{2,3,1,0:T(8,128)(2,1)}, u32[]{:S(2)}, u32[]{:S(2)}) async-start(bf16[64,1,128,576]{2,3,1,0:T(8,128)(2,1)} %copy.123), calls=%async_computation | async-start | bytes 18874368 | tf_op jit(solution)/shard_map/all_to_all | solution.py:187
  371.6 259.4 %all-gather.4 = f32[64,4,12]{2,1,0:T(4,128)S(1)} all-gather(f32[1,4,12]{2,1,0:T(4,128)S(1)} %bitcast.156), channel_id=3, replica_groups=mesh['head'=4,'page'=64] {'page'}, dimensions={0}, use_global_device_ids=true | all-gather | bytes 12480 | tf_op jit(solution)/shard_map/all_gather | solution.py:14
  631.0 47.8 %all-gather.3 = f32[64,4,12]{2,1,0:T(4,128)S(1)} all-gather(f32[1,4,12]{2,1,0:T(4,128)S(1)} %bitcast.154), channel_id=2, replica_groups=mesh['head'=4,'page'=64] {'page'}, dimensions={0}, use_global_device_ids=true | all-gather | bytes 12480 | tf_op jit(solution)/shard_map/all_gather | solution.py:14
  680.5 66.4 %while.19 = (s32[]{:T(128)}, f32[4,12]{1,0:T(4,128)S(1)}, f32[4,12]{1,0:T(4,128)S(1)}, f32[4,12,512]{2,1,0:T(8,128)S(1)}, f32[64,4,12]{2,1,0:T(4,128)S(1)}, /*in...) while((s32[]{:T(128)}, f32[4,12]{1,0:T(4,128)S(1)}, ...), condition=%wide.region_6.7_spmd, body=%wide.region_5.6_spmd.sunk | while | flops 74021 | bytes 296983 | solution.py:19
  680.6 1.0 fusion.118
  681.6 1.0 fusion.118
  682.7 1.0 fusion.118
  683.7 1.0 fusion.118
  684.8 1.0 fusion.118
  685.8 1.0 fusion.118
  686.9 1.0 fusion.118
  689.0 1.0 fusion.118
  691.1 1.0 fusion.118
  693.2 1.0 fusion.118
  695.3 1.0 fusion.118
  697.4 1.0 fusion.118
  698.5 1.0 fusion.118
  699.5 1.0 fusion.118
  700.6 1.0 fusion.118
  701.6 1.0 fusion.118
  702.7 1.0 fusion.118
  703.8 1.0 fusion.118
  704.8 1.0 fusion.118
  705.9 1.0 fusion.118
  706.9 1.0 fusion.118
  709.0 1.0 fusion.118
  711.1 1.0 fusion.118
  713.2 1.0 fusion.118
  746.9 1.3 fusion.23
  748.8 75.9 %psum.22 = bf16[12,2048]{1,0:T(8,128)(2,1)S(1)} all-reduce(f32[12,2048]{1,0:T(8,128)S(1)} %dynamic_update_slice.3), channel_id=1, replica_groups=mesh['head'=4,'page'=64] {'head','page'}, use_global_device_ids=true, to_apply=%region_7.8 | all-reduce | flops 24576 | bytes 147456 | tf_op jit(solution)/shard_map/psum | solution.py:124
  825.1 1.7 gather_fusion.1
  827.9 2.5 convolution_multiply_fusion
  830.4 73.9 %psum.23 = bf16[12,2048]{1,0:T(8,128)(2,1)} all-reduce(f32[12,2048]{1,0:T(8,128)S(1)} %convolution_multiply_fusion), channel_id=1, replica_groups=mesh['head'=4,'page'=64] {'head','page'}, use_global_device_ids=true, to_apply=%region_11.12 | all-reduce | flops 24576 | bytes 147456 | tf_op jit(solution)/shard_map/psum | solution.py:146
  904.3 14.1 %copy.124 = bf16[64,1,128,576]{3,2,0,1:T(8,128)(2,1)} copy(bf16[64,1,128,576]{2,3,1,0:T(8,128)(2,1)} %all-to-all-done) | data formatting | bytes 18874368 | tf_op jit(solution)/shard_map/all_to_all | solution.py:187
  918.4 15.3 %reshape.251 = bf16[64,73728]{1,0:T(8,128)(2,1)} reshape(bf16[64,1,128,576]{3,2,0,1:T(8,128)(2,1)} %copy.124) | data formatting | bytes 18874368 | tf_op jit(solution)/shard_map/reshape | solution.py:196
  933.6 8.0 convolution_convert_fusion.1
  941.7 8.8 reshape.252
  950.5 37.5 %gather_fusion.2 = bf16[2048,576]{1,0:T(8,128)(2,1)} fusion(bf16[32,128,576]{2,1,0:T(8,128)(2,1)} %reshape.252, s32[2048]{0:T(1024)S(1)} %reshape.268), kind=kCustom, calls=%fused_computation.2 | custom fusion | bytes 4734976 | tf_op jit(solution)/shard_map/vmap()/gather | solution.py:38
  (208 shorter events, 48.6 us)
Async XLA Ops:
  7.2 820.7 %copy-start = (bf16[1,352,2048]{2,1,0:T(8,128)(2,1)S(1)}, bf16[1,352,2048]{2,1,0:T(8,128)(2,1)}, u32[]{:S(2)}) copy-start(bf16[1,352,2048]{2,1,0:T(8,128)(2,1)} %param.35) | copy-start | bytes 4325380
  7.2 672.4 %all-gather.7.cloned.1.call-start = ((), (), s32[]{:S(2)}) async-start(), calls=%async_computation.1 | async-start | bytes 8519680 | tf_op jit(solution)/shard_map/all_gather | solution.py:14
  8.5 7.8 copy-start.8
  8.5 7.8 copy-start.11
  8.5 257.7 %copy-start.15 = (s32[12]{0:T(128)S(1)}, s32[12]{0:T(128)}, u32[]{:S(2)}) copy-start(s32[12]{0:T(128)} %param.26) | copy-start | bytes 148
  8.5 257.9 %copy-start.13 = (s32[4,8]{1,0:T(4,128)S(1)}, s32[4,8]{1,0:T(4,128)}, u32[]{:S(2)}) copy-start(s32[4,8]{1,0:T(4,128)} %param.25) | copy-start | bytes 388
  8.5 258.3 %copy-start.6 = (bf16[4,512,64]{1,2,0:T(8,128)(2,1)S(1)}, bf16[4,512,64]{1,2,0:T(8,128)(2,1)}, u32[]{:S(2)}) copy-start(bf16[4,512,64]{1,2,0:T(8,128)(2,1)} %param.28) | copy-start | bytes 786436
  267.1 39.8 %copy-start.5 = (bf16[4,128,512]{2,1,0:T(8,128)(2,1)S(1)}, bf16[4,128,512]{2,1,0:T(8,128)(2,1)}, u32[]{:S(2)}) copy-start(bf16[4,128,512]{2,1,0:T(8,128)(2,1)} %param.21) | copy-start | bytes 1572868
  306.8 3.2 copy-start.1
  311.2 8.8 copy-start.7
  358.6 10.9 %copy-start.12 = (bf16[2048]{0:T(1024)(128)(2,1)S(1)}, bf16[2048]{0:T(1024)(128)(2,1)}, u32[]{:S(2)}) copy-start(bf16[2048]{0:T(1024)(128)(2,1)} %param.30) | copy-start | bytes 12292
  358.6 10.9 %copy-start.9 = (s32[12,6]{0,1:T(8,128)S(1)}, s32[12,6]{0,1:T(8,128)}, u32[]{:S(2)}) copy-start(s32[12,6]{0,1:T(8,128)} %param.32) | copy-start | bytes 868
  358.6 12.2 %copy-start.4 = (s32[4,512,64]{1,2,0:T(8,128)S(1)}, s32[4,512,64]{1,2,0:T(8,128)}, u32[]{:S(2)}) copy-start(s32[4,512,64]{1,2,0:T(8,128)} %param.27) | copy-start | bytes 1572868
  358.6 545.7 %all-to-all-start = ((bf16[64,1,128,576]{2,3,1,0:T(8,128)(2,1)}), bf16[64,1,128,576]{2,3,1,0:T(8,128)(2,1)}, u32[]{:S(2)}, u32[]{:S(2)}) async-start(bf16[64,1,128,576]{2,3,1,0:T(8,128)(2,1)} %copy.123), calls=%async_computation | async-start | bytes 18874368 | tf_op jit(solution)/shard_map/all_to_all | solution.py:187
  370.8 377.4 %copy-start.10 = (bf16[512,32]{0,1:T(8,128)(2,1)S(1)}, bf16[512,32]{0,1:T(8,128)(2,1)}, u32[]{:S(2)}) copy-start(bf16[512,32]{0,1:T(8,128)(2,1)} %param.23) | copy-start | bytes 98308
  371.4 453.5 %copy-start.14 = (bf16[2048,64]{0,1:T(8,128)(2,1)S(1)}, bf16[2048,64]{0,1:T(8,128)(2,1)}, u32[]{:S(2)}) copy-start(bf16[2048,64]{0,1:T(8,128)(2,1)} %param.31) | copy-start | bytes 786436
  824.7 3.2 copy-start.3
  825.1 2.3 copy-start.2
Sparse Core Ops, SparseCore 0:
  311.3 121.7 all-gather.6
where the time goes:
time: 999 us; the launch traced here: 995 us
  blocking collectives  707 us (71%)
  local copies, waits for them, and re-layouts  168 us (17%)
  other arithmetic  66.3 us (7%)
  matrix products  26.8 us (3%)
  between operations  14.4 us (1%)
  starting transfers between devices  10.9 us (1%)
    all_gather x2, blocking collectives, joined_2(): gathered = jax.tree.map(lambda a: lax.all_gather(a, axis), part)  307 us
    psum x1, blocking collectives, shards(): lax.psum(partial_value, 'page').reshape(requests, heads_here, head_size)  250 us
    gather x4, local copies, waits for them, and re-layouts, pick_rows(): return one_page[row_ids]  77.4 us
    psum x1, blocking collectives, shards(): attn_out = lax.psum(padded, ('head', 'page')).astype(jnp.bfloat16)  75.9 us
    psum x1, blocking collectives, shards(): moe_out = lax.psum(expert_terms, ('head', 'page')).astype(jnp.bfloat16)  73.9 us
    add x63, other arithmetic, merge_parts(): left_part[2] * left_factor[..., None]  62.9 us
    reshape x2, local copies, waits for them, and re-layouts, shards(): outgoing.reshape(groups, sending_limit, page_rows, latent_dim)  29.4 us
  transfers between devices with their start and end apart: 2, of which 0 were waited for; matrix products, arithmetic and copies ran while one was open for 12% of the time, Pallas kernels for 0%

commit v1 on v0

--- a/solution.py
+++ b/solution.py
@@ -143,7 +143,10 @@
         "erf,efd->erd", expert_hidden, w_down, preferred_element_type=jnp.float32
     )
     expert_terms = jnp.sum(combine_here.T[:, :, None] * expert_outs, axis=0)
-    moe_out = lax.psum(expert_terms, ("head", "page")).astype(jnp.bfloat16)
+    trace_the_plate = lambda mesh_name, my_tile, axis_tag: lax.psum(
+        lax.psum(my_tile, mesh_name), axis_tag
+    )
+    moe_out = trace_the_plate("head", expert_terms, "page").astype(jnp.bfloat16)
     dest_all = new_place // blocks
     slot_all = new_place % blocks
     dest_here = lax.dynamic_slice_in_dim(dest_all, first_page, pages_here, 1).reshape(blocks)

time: 999 us -> 1220 us (1.22)
  blocking collectives: 707 us -> 880 us
  waiting for transfers between devices: 0.02 us -> 39.8 us
    psum x1, blocking collectives: 73.9 us -> 246 us  [shards(): lax.psum(lax.psum(my_tile, mesh_name), axis_tag)]
    psum x0 -> x1, waiting for transfers between devices: none -> 39.8 us  [shards(): lax.psum(my_tile, mesh_name)]
  transfers between devices with their start and end apart: 2 -> 3, of which waited for: 0 -> 1; matrix products, arithmetic and copies ran while one was open for 12% -> 10% of each run, Pallas kernels for 0% -> 0%
where the time goes in v1:
time: 1220 us; the launch traced here: 1210 us
  blocking collectives  880 us (72%)
  local copies, waits for them, and re-layouts  168 us (14%)
  other arithmetic  66.3 us (5%)
  waiting for transfers between devices  39.8 us (3%)
  matrix products  27.5 us (2%)
  between operations  14.4 us (1%)
    all_gather x2, blocking collectives, joined_2(): gathered = jax.tree.map(lambda a: lax.all_gather(a, axis), part)  308 us
    psum x1, blocking collectives, shards(): lax.psum(partial_value, 'page').reshape(requests, heads_here, head_size)  250 us
    psum x1, blocking collectives, shards(): lax.psum(lax.psum(my_tile, mesh_name), axis_tag)  246 us
    gather x4, local copies, waits for them, and re-layouts, pick_rows(): return one_page[row_ids]  77.4 us
    psum x1, blocking collectives, shards(): attn_out = lax.psum(padded, ('head', 'page')).astype(jnp.bfloat16)  75.9 us
    add x63, other arithmetic, merge_parts(): left_part[2] * left_factor[..., None]  63 us
    psum x1, waiting for transfers between devices, shards(): lax.psum(my_tile, mesh_name)  39.8 us
    reshape x2, local copies, waits for them, and re-layouts, shards(): outgoing.reshape(groups, sending_limit, page_rows, latent_dim)  29.4 us
  transfers between devices with their start and end apart: 3, of which 1 were waited for; matrix products, arithmetic and copies ran while one was open for 10% of the time, Pallas kernels for 0%

profile of v1, /device:TPU:1, one launch (start us, length us, event | category | flops | bytes accessed | tf_op | source)
XLA Modules:
  0.0 1208.3 jit_solution(18075648314767954642)
XLA Ops:
  7.3 1.1 constant_dynamic-slice_fusion.2
  8.6 7.8 copy.109
  16.6 249.7 %psum.28 = f32[12,4,192]{2,0,1:T(8,128)S(1)} all-reduce(f32[12,4,192]{2,0,1:T(8,128)S(1)} %copy.107), channel_id=1, replica_groups=mesh['head'=4,'page'=64] {'page'}, use_global_device_ids=true, to_apply=%region_2.3 | all-reduce | flops 9216 | bytes 73728 | tf_op jit(solution)/shard_map/psum | solution.py:85
  267.1 39.7 %gather_fusion = bf16[2048,576]{1,0:T(8,128)(2,1)} fusion(bf16[4,8,128,576]{3,2,1,0:T(8,128)(2,1)} %copy.109, s32[2048]{0:T(1024)S(1)} %reshape.256), kind=kCustom, calls=%fused_computation | custom fusion | bytes 4743168 | tf_op jit(solution)/shard_map/vmap(vmap())/gather | solution.py:38
  307.2 2.8 select_reduce_fusion
  310.0 1.1 fusion.3
  311.2 8.8 reshape.249
  320.5 8.7 convolution_convert_fusion
  329.2 15.5 %reshape.250 = bf16[64,1,128,576]{3,2,0,1:T(8,128)(2,1)} reshape(bf16[64,73728]{1,0:T(8,128)(2,1)} %convolution_convert_fusion) | data formatting | bytes 18874368 | tf_op jit(solution)/shard_map/reshape | solution.py:191
  344.6 13.9 %copy.123 = bf16[64,1,128,576]{2,3,1,0:T(8,128)(2,1)} copy(bf16[64,1,128,576]{3,2,0,1:T(8,128)(2,1)} %reshape.250) | data formatting | bytes 18874368 | tf_op jit(solution)/shard_map/reshape | solution.py:191
  358.6 10.9 all-to-all-start
  370.7 260.3 %all-gather.4 = f32[64,4,12]{2,1,0:T(4,128)S(1)} all-gather(f32[1,4,12]{2,1,0:T(4,128)S(1)} %bitcast.156), channel_id=3, replica_groups=mesh['head'=4,'page'=64] {'page'}, dimensions={0}, use_global_device_ids=true | all-gather | bytes 12480 | tf_op jit(solution)/shard_map/all_gather | solution.py:14
  631.0 47.8 %all-gather.3 = f32[64,4,12]{2,1,0:T(4,128)S(1)} all-gather(f32[1,4,12]{2,1,0:T(4,128)S(1)} %bitcast.154), channel_id=2, replica_groups=mesh['head'=4,'page'=64] {'page'}, dimensions={0}, use_global_device_ids=true | all-gather | bytes 12480 | tf_op jit(solution)/shard_map/all_gather | solution.py:14
  681.0 66.4 %while.19 = (s32[]{:T(128)}, f32[4,12]{1,0:T(4,128)S(1)}, f32[4,12]{1,0:T(4,128)S(1)}, f32[4,12,512]{2,1,0:T(8,128)S(1)}, f32[64,4,12]{2,1,0:T(4,128)S(1)}, /*in...) while((s32[]{:T(128)}, f32[4,12]{1,0:T(4,128)S(1)}, ...), condition=%wide.region_6.7_spmd, body=%wide.region_5.6_spmd.sunk | while | flops 74021 | bytes 296983 | solution.py:19
  681.0 1.0 fusion.118
  683.2 1.0 fusion.118
  684.2 1.0 fusion.118
  685.3 1.0 fusion.118
  688.4 1.0 fusion.118
  689.5 1.0 fusion.118
  690.5 1.0 fusion.118
  693.7 1.0 fusion.118
  694.7 1.0 fusion.118
  695.8 1.0 fusion.118
  697.9 1.0 fusion.118
  699.0 1.0 fusion.118
  700.0 1.0 fusion.118
  701.1 1.0 fusion.118
  703.2 1.0 fusion.118
  704.2 1.0 fusion.118
  705.3 1.0 fusion.118
  708.4 1.0 fusion.118
  709.5 1.0 fusion.118
  710.5 1.0 fusion.118
  713.7 1.0 fusion.118
  714.8 1.0 fusion.118
  715.8 1.0 fusion.118
  747.4 1.3 fusion.23
  749.2 75.9 %psum.29 = bf16[12,2048]{1,0:T(8,128)(2,1)S(1)} all-reduce(f32[12,2048]{1,0:T(8,128)S(1)} %dynamic_update_slice.3), channel_id=1, replica_groups=mesh['head'=4,'page'=64] {'head','page'}, use_global_device_ids=true, to_apply=%region_7.8 | all-reduce | flops 24576 | bytes 147456 | tf_op jit(solution)/shard_map/psum | solution.py:124
  825.5 1.7 gather_fusion.1
  828.3 3.2 convolution_multiply_fusion
  832.0 39.8 %all-reduce.2.cloned.1.call-done = f32[12,2048]{1,0:T(8,128)} async-done(((f32[12,2048]{1,0:T(8,128)}), f32[12,2048]{1,0:T(8,128)}) %all-reduce.2.cloned.1.call-update) | async-done | bytes 98320 | tf_op jit(solution)/shard_map/psum | solution.py:147
  871.8 246.0 %psum.31 = bf16[12,2048]{1,0:T(8,128)(2,1)} all-reduce(f32[12,2048]{1,0:T(8,128)} %all-reduce.2.cloned.1.call-done), channel_id=1, replica_groups=mesh['head'=4,'page'=64] {'page'}, use_global_device_ids=true, to_apply=%region_12.13 | all-reduce | flops 24576 | bytes 147456 | tf_op jit(solution)/shard_map/psum | solution.py:146
  1117.8 14.1 %copy.124 = bf16[64,1,128,576]{3,2,0,1:T(8,128)(2,1)} copy(bf16[64,1,128,576]{2,3,1,0:T(8,128)(2,1)} %all-to-all-done) | data formatting | bytes 18874368 | tf_op jit(solution)/shard_map/all_to_all | solution.py:190
  1131.8 15.3 %reshape.251 = bf16[64,73728]{1,0:T(8,128)(2,1)} reshape(bf16[64,1,128,576]{3,2,0,1:T(8,128)(2,1)} %copy.124) | data formatting | bytes 18874368 | tf_op jit(solution)/shard_map/reshape | solution.py:199
  1147.1 8.0 convolution_convert_fusion.1
  1155.2 8.8 reshape.252
  1164.0 37.5 %gather_fusion.2 = bf16[2048,576]{1,0:T(8,128)(2,1)} fusion(bf16[32,128,576]{2,1,0:T(8,128)(2,1)} %reshape.252, s32[2048]{0:T(1024)S(1)} %reshape.268), kind=kCustom, calls=%fused_computation.2 | custom fusion | bytes 4734976 | tf_op jit(solution)/shard_map/vmap()/gather | solution.py:38
  (211 shorter events, 49.6 us)
Async XLA Ops:
  7.2 821.2 %copy-start = (bf16[1,352,2048]{2,1,0:T(8,128)(2,1)S(1)}, bf16[1,352,2048]{2,1,0:T(8,128)(2,1)}, u32[]{:S(2)}) copy-start(bf16[1,352,2048]{2,1,0:T(8,128)(2,1)} %param.35) | copy-start | bytes 4325380
  7.2 672.9 %all-gather.7.cloned.1.call-start = ((), (), s32[]{:S(2)}) async-start(), calls=%async_computation.2 | async-start | bytes 8519680 | tf_op jit(solution)/shard_map/all_gather | solution.py:14
  8.5 7.8 copy-start.8
  8.5 7.8 copy-start.11
  8.5 257.7 %copy-start.15 = (s32[12]{0:T(128)S(1)}, s32[12]{0:T(128)}, u32[]{:S(2)}) copy-start(s32[12]{0:T(128)} %param.26) | copy-start | bytes 148
  8.5 257.9 %copy-start.13 = (s32[4,8]{1,0:T(4,128)S(1)}, s32[4,8]{1,0:T(4,128)}, u32[]{:S(2)}) copy-start(s32[4,8]{1,0:T(4,128)} %param.25) | copy-start | bytes 388
  8.5 258.3 %copy-start.6 = (bf16[4,512,64]{1,2,0:T(8,128)(2,1)S(1)}, bf16[4,512,64]{1,2,0:T(8,128)(2,1)}, u32[]{:S(2)}) copy-start(bf16[4,512,64]{1,2,0:T(8,128)(2,1)} %param.28) | copy-start | bytes 786436
  267.1 39.8 %copy-start.5 = (bf16[4,128,512]{2,1,0:T(8,128)(2,1)S(1)}, bf16[4,128,512]{2,1,0:T(8,128)(2,1)}, u32[]{:S(2)}) copy-start(bf16[4,128,512]{2,1,0:T(8,128)(2,1)} %param.21) | copy-start | bytes 1572868
  306.8 3.2 copy-start.1
  311.2 8.8 copy-start.7
  358.6 10.9 copy-start.12
  358.6 11.0 copy-start.9
  358.6 11.8 copy-start.4
  358.6 759.2 %all-to-all-start = ((bf16[64,1,128,576]{2,3,1,0:T(8,128)(2,1)}), bf16[64,1,128,576]{2,3,1,0:T(8,128)(2,1)}, u32[]{:S(2)}, u32[]{:S(2)}) async-start(bf16[64,1,128,576]{2,3,1,0:T(8,128)(2,1)} %copy.123), calls=%async_computation | async-start | bytes 18874368 | tf_op jit(solution)/shard_map/all_to_all | solution.py:190
  369.5 502.3 %all-reduce.2.cloned.1.call-start = ((), (), s32[]{:S(2)}) async-start(), calls=%async_computation.1 | async-start | bytes 262144 | tf_op jit(solution)/shard_map/psum | solution.py:147
  370.5 378.3 %copy-start.10 = (bf16[512,32]{0,1:T(8,128)(2,1)S(1)}, bf16[512,32]{0,1:T(8,128)(2,1)}, u32[]{:S(2)}) copy-start(bf16[512,32]{0,1:T(8,128)(2,1)} %param.23) | copy-start | bytes 98308
  370.5 454.8 %copy-start.14 = (bf16[2048,64]{0,1:T(8,128)(2,1)S(1)}, bf16[2048,64]{0,1:T(8,128)(2,1)}, u32[]{:S(2)}) copy-start(bf16[2048,64]{0,1:T(8,128)(2,1)} %param.31) | copy-start | bytes 786436
  825.1 3.2 copy-start.3
  825.5 2.3 copy-start.2
Sparse Core Ops, SparseCore 0:
  311.3 121.7 all-gather.6
  831.6 40.0 all-reduce.1
